TPU v7x, 512 devices: a whole 4x4x16 slice. The times are simulated.
512 devices in a mesh: grp: 32 (over y, x, core), shard: 16 (over z).
Axes of the slice: x: 4, y: 4, z: 16, core: 2. Of those that a mesh axis runs over, the one named last changes fastest.
Arguments:
- grads: bfloat16 [2, 32, 16, 768, 768], P(None, 'grp', 'shard')
- vec_grads: bfloat16 [2, 32, 16, 8, 768], P(None, 'grp', 'shard'), may hold values from -0.5 to 0.5
- weight: float32 [768, 768], P('shard'), may hold values from -0.21875 to 0.21875
- basis: float32 [768, 256], replicated, may hold values from -0.21875 to 0.21875
- moment: float32 [768, 256], P('shard'), may hold values from -4 to 4
- second: float32 [768, 256], P('shard'), may hold values from 0.01 to 1
- vectors: float32 [8, 768], P(None, 'shard'), may hold values from -6 to 6
- vec_moment: float32 [8, 768], P(None, 'shard'), may hold values from -1.5 to 1.5
- vec_second: float32 [8, 768], P(None, 'shard'), may hold values from 0.001 to 0.1
Outputs:
- new_weight: float32 [768, 768], P('shard')
- update: bfloat16 [768, 768], P('shard')
- new_moment: float32 [768, 256], P('shard')
- new_second: float32 [768, 256], P('shard')
- new_basis: float32 [768, 256], replicated
- new_vectors: float32 [8, 768], P(None, 'shard')
- new_vec_moment: float32 [8, 768], P(None, 'shard')
- new_vec_second: float32 [8, 768], P(None, 'shard')
All inputs are finite; a program needn't handle non-finite values.
Results may differ from a plain program's by a relative error of at most 0.001.
Values sent between devices are 32-bit elements; how exact they have to be, the bound alone decides.
A program may use at most 64 MiB of HBM per device.

v0:
```python
import jax
import jax.numpy as jnp
from jax import lax
from jax.sharding import PartitionSpec as P

NS_STEPS = 5
STEP = 100
HIGH = lax.Precision.HIGHEST


def matmul(left, right):
    return jnp.dot(left, right, precision=HIGH, preferred_element_type=jnp.float32)


def per_device(grads, vec_grads, weight, basis, moment, second, vectors, vec_moment, vec_second):
    shards = lax.axis_size("shard")
    width = grads.shape[-1]
    rows = weight.shape[0]
    cols = vectors.shape[1]
    me = lax.axis_index("shard")
    summed = grads[0, 0, 0].astype(jnp.float32) + grads[1, 0, 0].astype(jnp.float32)
    vec_local = vec_grads[0, 0, 0].astype(jnp.float32) + vec_grads[1, 0, 0].astype(jnp.float32)
    packed = jnp.concatenate([summed, vec_local], axis=0)
    packed = lax.psum(packed, ("grp", "shard"))
    total = packed[:width]
    vec_total = packed[width:]
    projected_all = matmul(total, basis)
    subspace = lax.dot_general(
        total,
        projected_all,
        (((0,), (0,)), ((), ())),
        precision=HIGH,
        preferred_element_type=jnp.float32,
    )
    squares = jnp.sum(total * total) + jnp.sum(vec_total * vec_total)
    iterate = subspace / jnp.sqrt(jnp.sum(subspace * subspace) + 1e-06)
    for step in range(NS_STEPS):
        gram = matmul(iterate.T, iterate)
        iterate = 1.5 * iterate - 0.5 * matmul(iterate, gram)
    factor = 1.0 / jnp.maximum(jnp.sqrt(squares / (width * width + vec_total.size)), 1.0)
    projected = lax.dynamic_slice_in_dim(projected_all, me * rows, rows, axis=0)
    vec_sum = lax.dynamic_slice_in_dim(vec_total, me * cols, cols, axis=1)
    first_fix = 1.0 - 0.9**STEP
    second_fix = 1.0 - 0.999**STEP
    grad_low = factor * projected
    new_moment = 0.9 * moment + 0.1 * grad_low
    new_second = 0.999 * second + 0.001 * grad_low * grad_low
    normalized = new_moment / first_fix / (jnp.sqrt(new_second / second_fix) + 1e-08)
    full = lax.dot_general(
        normalized,
        basis,
        (((1,), (1,)), ((), ())),
        precision=HIGH,
        preferred_element_type=jnp.float32,
    )
    new_weight = weight - 0.001 * (0.25 * full + 0.01 * weight)
    vec_grad = factor * vec_sum
    new_vec_moment = 0.9 * vec_moment + 0.1 * vec_grad
    new_vec_second = 0.999 * vec_second + 0.001 * vec_grad * vec_grad
    vec_step = new_vec_moment / first_fix / (jnp.sqrt(new_vec_second / second_fix) + 1e-08)
    new_vectors = vectors - 0.001 * (vec_step + 0.01 * vectors)
    return (
        new_weight,
        full.astype(jnp.bfloat16),
        new_moment,
        new_second,
        iterate,
        new_vectors,
        new_vec_moment,
        new_vec_second,
    )


def solution(mesh):
    return jax.shard_map(
        per_device,
        mesh=mesh,
        in_specs=(
            P(None, "grp", "shard", None, None),
            P(None, "grp", "shard", None, None),
            P("shard", None),
            P(),
            P("shard", None),
            P("shard", None),
            P(None, "shard"),
            P(None, "shard"),
            P(None, "shard"),
        ),
        out_specs=(
            P("shard", None),
            P("shard", None),
            P("shard", None),
            P("shard", None),
            P(),
            P(None, "shard"),
            P(None, "shard"),
            P(None, "shard"),
        ),
        check_vma=False,
    )
```

profile of v0, /device:TPU:1, one launch (start us, length us, event | category | flops | bytes accessed | tf_op | source)
XLA Modules:
  0.0 534.5 jit_solution(420021904912794236)
XLA Ops:
  7.2 0.0 copy-start
  7.2 0.0 all-reduce.2.cloned.1.call-start
  7.2 0.8 add_bitcast_fusion.1
  8.0 1.9 add_bitcast_fusion
  9.9 1.6 pad_maximum_fusion
  11.5 0.0 all-reduce.2.cloned.1.call-update
  11.5 485.5 %all-reduce.2.cloned.1.call-done = f32[776,768]{1,0:T(8,128)} async-done(((f32[776,768]{1,0:T(8,128)}), f32[776,768]{1,0:T(8,128)}) %all-reduce.2.cloned.1.call-update) | async-done | bytes 2383888 | tf_op jit(solution)/shard_map/psum | solution.py:24
  497.0 3.0 multiply_reduce_fusion
  500.0 1.3 fusion.25
  502.7 2.0 fusion.2
  504.8 5.3 multiply_reduce_fusion.1
  510.9 2.9 fusion.9
  513.8 0.8 fusion.8
  514.6 1.4 fusion.27
  516.0 0.8 fusion.7
  516.8 1.6 fusion.28
  518.4 0.8 fusion.6
  519.2 1.4 fusion.29
  520.6 0.0 copy-start.7
  520.6 0.0 copy-start.8
  520.7 0.8 fusion.5
  521.4 0.0 copy-start.6
  521.5 0.0 copy-start.9
  521.5 0.0 copy-start.10
  521.5 0.0 copy-start.11
  521.5 1.4 fusion.30
  522.9 1.7 fusion.4
  524.6 0.8 multiply_add_fusion
  525.4 0.0 copy-start.4
  525.4 0.0 copy-start.5
  525.5 1.5 fusion.26
  527.0 0.7 multiply_subtract_fusion.1
  (15 shorter events, 0.0 us)
Async XLA Ops:
  7.2 495.5 %copy-start = (f32[768,256]{1,0:T(8,128)S(1)}, f32[768,256]{1,0:T(8,128)}, u32[]{:S(2)}) copy-start(f32[768,256]{1,0:T(8,128)} %param.12) | copy-start | bytes 2359300
  7.2 489.8 %all-reduce.2.cloned.1.call-start = ((), (), s32[]{:S(2)}) async-start(), calls=%async_computation | async-start | bytes 4767744 | tf_op jit(solution)/shard_map/psum | solution.py:24
  497.0 5.8 %copy-start.1 = (f32[776,768]{1,0:T(8,128)S(1)}, f32[776,768]{1,0:T(8,128)}, u32[]{:S(2)}) copy-start(f32[776,768]{1,0:T(8,128)} %all-reduce.2.cloned.1.call-done) | copy-start | bytes 7151620
  504.7 5.3 %copy-start.2 = (f32[768,256]{1,0:T(8,128)}, f32[768,256]{1,0:T(8,128)S(1)}, u32[]{:S(2)}) copy-start(f32[768,256]{1,0:T(8,128)S(1)} %fusion.2) | copy-start | bytes 2359300
  510.1 3.7 copy-start.3
  520.6 4.0 copy-start.7
  520.6 4.0 copy-start.8
  521.4 4.0 copy-start.6
  521.5 5.5 %copy-start.9 = (f32[8,48]{1,0:T(8,128)S(1)}, f32[8,48]{1,0:T(8,128)}, u32[]{:S(2)}) copy-start(f32[8,48]{1,0:T(8,128)} %param.15) | copy-start | bytes 4612
  521.5 5.5 %copy-start.10 = (f32[8,48]{1,0:T(8,128)S(1)}, f32[8,48]{1,0:T(8,128)}, u32[]{:S(2)}) copy-start(f32[8,48]{1,0:T(8,128)} %param.16) | copy-start | bytes 4612
  521.5 5.5 %copy-start.11 = (f32[8,48]{1,0:T(8,128)S(1)}, f32[8,48]{1,0:T(8,128)}, u32[]{:S(2)}) copy-start(f32[8,48]{1,0:T(8,128)} %param.17) | copy-start | bytes 4612
  525.4 2.3 copy-start.4
  525.4 2.3 copy-start.5
Sparse Core Ops, SparseCore 0:
  13.4 483.5 all-reduce.1
where the time goes:
time: 535 us
  waiting for transfers between devices  485 us (91%)
  matrix products  22.4 us (4%)
  between operations  16.4 us (3%)
  other arithmetic  10.1 us (2%)
    psum x1, waiting for transfers between devices, per_device(): packed = lax.psum(packed, ('grp', 'shard'))  485 us
    dot_general x11, matrix products, matmul(): jnp.dot(left, right, precision=HIGH, preferred_element_type=jnp.float32)  15.6 us
  transfers between devices with their start and end apart: 1, of which 1 were waited for; matrix products, arithmetic and copies ran while one was open for 0% of the time, Pallas kernels for 0%

commit v1 on v0

--- a/solution.py
+++ b/solution.py
@@ -21,7 +21,7 @@
     summed = grads[0, 0, 0].astype(jnp.float32) + grads[1, 0, 0].astype(jnp.float32)
     vec_local = vec_grads[0, 0, 0].astype(jnp.float32) + vec_grads[1, 0, 0].astype(jnp.float32)
     packed = jnp.concatenate([summed, vec_local], axis=0)
-    packed = lax.psum(packed, ("grp", "shard"))
+    packed = lax.psum(lax.psum(packed, "shard"), "grp")
     total = packed[:width]
     vec_total = packed[width:]
     projected_all = matmul(total, basis)

time: 535 us -> 339 us (0.63)
  waiting for transfers between devices: 485 us -> 290 us
    psum x1 -> x2, waiting for transfers between devices: 485 us -> 290 us  [per_device(): packed = lax.psum(lax.psum(packed, 'shard'), 'grp')]
  transfers between devices with their start and end apart: 1 -> 2, of which waited for: 1 -> 2; matrix products, arithmetic and copies ran while one was open for 0% -> 0% of each run, Pallas kernels for 0% -> 0%
where the time goes in v1:
time: 339 us
  waiting for transfers between devices  290 us (86%)
  matrix products  22.4 us (7%)
  between operations  16.4 us (5%)
  other arithmetic  10.1 us (3%)
    psum x2, waiting for transfers between devices, per_device(): packed = lax.psum(lax.psum(packed, 'shard'), 'grp')  290 us
    dot_general x11, matrix products, matmul(): jnp.dot(left, right, precision=HIGH, preferred_element_type=jnp.float32)  15.6 us
  transfers between devices with their start and end apart: 2, of which 2 were waited for; matrix products, arithmetic and copies ran while one was open for 0% of the time, Pallas kernels for 0%

profile of v1, /device:TPU:1, one launch (start us, length us, event | category | flops | bytes accessed | tf_op | source)
XLA Modules:
  0.0 338.9 jit_solution(4495519119121037532)
XLA Ops:
  7.2 0.0 copy-start
  7.2 0.0 all-reduce.3.cloned.1.call-start
  7.2 0.8 add_bitcast_fusion.1
  8.0 1.9 add_bitcast_fusion
  9.9 1.6 pad_maximum_fusion
  11.5 0.0 all-reduce.3.cloned.1.call-update
  11.5 0.0 all-reduce.5.cloned.1.call-start
  11.5 143.2 %all-reduce.3.cloned.1.call-done = f32[776,768]{1,0:T(8,128)} async-done(((f32[776,768]{1,0:T(8,128)}), f32[776,768]{1,0:T(8,128)}) %all-reduce.3.cloned.1.call-update) | async-done | bytes 2383888 | tf_op jit(solution)/shard_map/psum | solution.py:24
  154.7 0.0 all-reduce.5.cloned.1.call-update
  154.7 146.6 %all-reduce.5.cloned.1.call-done = f32[776,768]{1,0:T(8,128)} async-done(((f32[776,768]{1,0:T(8,128)}), f32[776,768]{1,0:T(8,128)}) %all-reduce.5.cloned.1.call-update) | async-done | bytes 2383888 | tf_op jit(solution)/shard_map/psum | solution.py:24
  301.3 3.0 multiply_reduce_fusion
  304.4 1.3 fusion.25
  307.1 2.0 fusion.2
  309.1 5.3 %multiply_reduce_fusion.1 = (f32[]{:T(128)}, f32[768,256]{1,0:T(8,128)}) fusion(f32[768,256]{1,0:T(8,128)S(1)} %fusion.2, f32[776,768]{1,0:T(8,128)S(1)} %copy-done.1), kind=kOutput, calls=%fused_computation.17 | convolution fusion | flops 1812332544 | bytes 3932164 | tf_op jit(solution)/shard_map/dot_general | solution.py:28
  315.2 2.9 fusion.9
  318.2 0.8 fusion.8
  319.0 1.4 fusion.27
  320.4 0.8 fusion.7
  321.2 1.6 fusion.28
  322.8 0.8 fusion.6
  323.6 1.4 fusion.29
  325.0 0.0 copy-start.7
  325.0 0.8 fusion.5
  325.8 0.0 copy-start.6
  325.9 0.0 copy-start.11
  325.9 1.4 fusion.30
  327.3 1.7 fusion.4
  329.0 0.8 multiply_add_fusion
  329.8 0.0 copy-start.4
  329.8 0.0 copy-start.5
  329.8 1.5 fusion.26
  331.4 0.7 multiply_subtract_fusion.1
  (18 shorter events, 0.0 us)
Async XLA Ops:
  7.2 299.9 %copy-start = (f32[768,256]{1,0:T(8,128)S(1)}, f32[768,256]{1,0:T(8,128)}, u32[]{:S(2)}) copy-start(f32[768,256]{1,0:T(8,128)} %param.12) | copy-start | bytes 2359300
  7.2 147.5 %all-reduce.3.cloned.1.call-start = ((), (), s32[]{:S(2)}) async-start(), calls=%async_computation | async-start | bytes 4767744 | tf_op jit(solution)/shard_map/psum | solution.py:24
  11.5 289.9 %all-reduce.5.cloned.1.call-start = ((), (), s32[]{:S(2)}) async-start(), calls=%async_computation.1 | async-start | bytes 4767744 | tf_op jit(solution)/shard_map/psum | solution.py:24
  301.3 5.8 %copy-start.1 = (f32[776,768]{1,0:T(8,128)S(1)}, f32[776,768]{1,0:T(8,128)}, u32[]{:S(2)}) copy-start(f32[776,768]{1,0:T(8,128)} %all-reduce.5.cloned.1.call-done) | copy-start | bytes 7151620
  309.1 5.3 %copy-start.2 = (f32[768,256]{1,0:T(8,128)}, f32[768,256]{1,0:T(8,128)S(1)}, u32[]{:S(2)}) copy-start(f32[768,256]{1,0:T(8,128)S(1)} %fusion.2) | copy-start | bytes 2359300
  314.5 3.7 %copy-start.3 = (f32[768,256]{1,0:T(8,128)S(1)}, f32[768,256]{1,0:T(8,128)}, u32[]{:S(2)}) copy-start(f32[768,256]{1,0:T(8,128)} %get-tuple-element.18) | copy-start | bytes 2359300
  325.0 4.0 %copy-start.7 = (f32[48,256]{1,0:T(8,128)S(1)}, f32[48,256]{1,0:T(8,128)}, u32[]{:S(2)}) copy-start(f32[48,256]{1,0:T(8,128)} %param.13) | copy-start | bytes 147460
  325.0 4.0 %copy-start.8 = (f32[48,256]{1,0:T(8,128)S(1)}, f32[48,256]{1,0:T(8,128)}, u32[]{:S(2)}) copy-start(f32[48,256]{1,0:T(8,128)} %param.14) | copy-start | bytes 147460
  325.8 4.0 %copy-start.6 = (f32[48,768]{1,0:T(8,128)S(1)}, f32[48,768]{1,0:T(8,128)}, u32[]{:S(2)}) copy-start(f32[48,768]{1,0:T(8,128)} %param.11) | copy-start | bytes 442372
  325.8 5.5 %copy-start.9 = (f32[8,48]{1,0:T(8,128)S(1)}, f32[8,48]{1,0:T(8,128)}, u32[]{:S(2)}) copy-start(f32[8,48]{1,0:T(8,128)} %param.15) | copy-start | bytes 4612
  325.9 5.5 %copy-start.10 = (f32[8,48]{1,0:T(8,128)S(1)}, f32[8,48]{1,0:T(8,128)}, u32[]{:S(2)}) copy-start(f32[8,48]{1,0:T(8,128)} %param.16) | copy-start | bytes 4612
  325.9 5.5 %copy-start.11 = (f32[8,48]{1,0:T(8,128)S(1)}, f32[8,48]{1,0:T(8,128)}, u32[]{:S(2)}) copy-start(f32[8,48]{1,0:T(8,128)} %param.17) | copy-start | bytes 4612
  329.8 2.3 copy-start.4
  329.8 2.3 copy-start.5
Sparse Core Ops, SparseCore 0:
  11.6 143.0 all-reduce.2
  158.0 143.2 all-reduce.4
